TPU v7x, 32 devices: a whole 2x2x4 slice. The times are simulated.
32 devices in a mesh: groups: 2 (over y), sess: 4 (over z), inner: 2 (over x), rep: 2 (over core).
Axes of the slice: x: 2, y: 2, z: 4, core: 2. Of those that a mesh axis runs over, the one named last changes fastest.
Arguments:
- thinker_rows: bfloat16 [4096, 3584], P(('groups', 'sess', 'rep'), 'inner'), parts along dimension 0, may hold values from -6 to 6
- row_session: int32 [4096, 1], P(('groups', 'sess', 'rep')), parts along dimension 0, may hold values from 0 to 31; in each aligned block of 256 rows (0 to 255, 256 to 511, ...) at most 12 rows name the same one
- speaker_of: int32 [64], P('groups'), parts along dimension 0, may hold values from 0 to 7
- prompt_slot: int32 [16], P('groups'), parts along dimension 0, may hold values from 0 to 7, each once
- prompt_cache: bfloat16 [16, 1024, 1024], P(('groups', 'sess'), ('inner', 'rep')), parts along dimension 0, may hold values from -64 to 64
- proj_weight: bfloat16 [3584, 896], P('inner'), may hold values from -0.09375 to 0.09375
- attn_gain: bfloat16 [896], replicated, may hold values from 0.5 to 1.5
- q_weight: bfloat16 [896, 1536], replicated, may hold values from -0.1875 to 0.1875
- k_weight: bfloat16 [896, 512], replicated, may hold values from -0.625 to 0.625
- v_weight: bfloat16 [896, 512], replicated, may hold values from -0.1875 to 0.1875
- o_weight: bfloat16 [1536, 896], replicated, may hold values from -0.15625 to 0.15625
Outputs:
- voice_states: bfloat16 [64, 96, 896], P(('groups', 'sess', 'inner', 'rep')), parts along dimension 0
There are 2 independent parts, one for each index of `groups`. A program takes and returns all parts, laid end to end along the dimension named above; an argument that names none is the same for every part. Nothing has to cross between parts.
Inputs may be any that keep to these rules, and one draw needn't show every extreme that they name: `row_session`: column 0 names the session of the row. Within each block of 256 rows (rows b * 256 to (b + 1) * 256 - 1, the rows of one index of sess+rep) no session is named by more than 12 rows, a bound that some block reaches; every session is named by some row. `prompt_slot`: each slot holds exactly one speaker's prompt.
All inputs are finite; a program needn't handle non-finite values.
Results may differ from a plain program's by a relative error of at most 0.0071.
Values may be sent and summed in bfloat16 or wider, within the bound.
No kernel may reach another device: no remote copies, remote signals or barrier semaphores. Data moves between devices by JAX's collectives and lax.ppermute only.
A program may use at most 128 MiB of HBM per device.

v0:
```python
import jax
import jax.numpy as jnp
from jax import lax
from jax.sharding import PartitionSpec as P

H = 12
KVH = 4
HD = 128
PROMPT = 1024
SLOTS = 96
EPSILON = 1e-06
ROPE_BASE = 1000000.0


def rms_scale(states, gain):
    widened = states.astype(jnp.float32)
    factor = lax.rsqrt(jnp.mean(widened * widened, axis=-1, keepdims=True) + EPSILON)
    return (widened * factor * gain.astype(jnp.float32)).astype(jnp.bfloat16)


def rope_tables(slot_total):
    half_width = HD // 2
    inverse = ROPE_BASE ** (-(jnp.arange(half_width, dtype=jnp.float32) * 2.0) / HD)
    angles = (PROMPT + jnp.arange(slot_total)).astype(jnp.float32)[:, None] * inverse[None, :]
    cosine = jnp.concatenate([jnp.cos(angles), jnp.cos(angles)], axis=1)[:, None, :]
    sine_table = jnp.concatenate([jnp.sin(angles), jnp.sin(angles)], axis=1)[:, None, :]
    return (cosine, sine_table)


def rotate(vectors, cosine, sine_table):
    half_width = vectors.shape[-1] // 2
    turned = jnp.concatenate([-vectors[..., half_width:], vectors[..., :half_width]], axis=-1)
    return vectors * cosine + turned * sine_table


def attend(states, lengths, prompts, attn_gain, q_weight, k_weight, v_weight, o_weight):
    session_total, slot_total, model_width = states.shape
    flat_rows = states.reshape(session_total * slot_total, model_width)
    normed = rms_scale(flat_rows, attn_gain)
    cosine, sine_table = rope_tables(slot_total)
    query = rotate(
        jnp.dot(normed, q_weight, preferred_element_type=jnp.float32).reshape(
            session_total, slot_total, H, HD
        ),
        cosine,
        sine_table,
    ).astype(jnp.bfloat16)
    own_keys = rotate(
        jnp.dot(normed, k_weight, preferred_element_type=jnp.float32).reshape(
            session_total, slot_total, KVH, HD
        ),
        cosine,
        sine_table,
    ).astype(jnp.bfloat16)
    own_values = (
        jnp.dot(normed, v_weight, preferred_element_type=jnp.float32)
        .reshape(session_total, slot_total, KVH, HD)
        .astype(jnp.bfloat16)
    )
    prompt_keys = prompts[:, :, : KVH * HD].reshape(session_total, PROMPT, KVH, HD)
    prompt_values = prompts[:, :, KVH * HD :].reshape(session_total, PROMPT, KVH, HD)
    all_keys = jnp.concatenate([prompt_keys, own_keys], axis=1)
    all_values = jnp.concatenate([prompt_values, own_values], axis=1)
    key_place = jnp.arange(PROMPT + slot_total) - PROMPT
    query_place = jnp.arange(slot_total)
    allowed = (key_place[None, None, :] < 0) | (
        key_place[None, None, :] <= query_place[None, :, None]
    ) & (key_place[None, None, :] < lengths[:, None, None])
    per_group = H // KVH
    outputs = []
    for kv_head in range(KVH):
        query_group = query[:, :, kv_head * per_group : (kv_head + 1) * per_group]
        scores = jnp.einsum(
            "cqhd,ckd->chqk",
            query_group,
            all_keys[:, :, kv_head],
            preferred_element_type=jnp.float32,
        ) * HD ** (-0.5)
        scores = jnp.where(allowed[:, None], scores, -1e30)
        highest = jnp.max(scores, axis=-1, keepdims=True)
        powers = jnp.exp(scores - highest)
        weights = (powers / jnp.sum(powers, axis=-1, keepdims=True)).astype(jnp.bfloat16)
        outputs.append(
            jnp.einsum(
                "chqk,ckd->cqhd",
                weights,
                all_values[:, :, kv_head],
                preferred_element_type=jnp.float32,
            )
        )
    attended = (
        jnp.concatenate(outputs, axis=2)
        .reshape(session_total * slot_total, H * HD)
        .astype(jnp.bfloat16)
    )
    return flat_rows.astype(jnp.float32) + jnp.dot(
        attended, o_weight, preferred_element_type=jnp.float32
    )


def body(
    thinker_rows,
    row_session,
    speaker_of,
    prompt_slot,
    prompt_cache,
    proj_weight,
    attn_gain,
    q_weight,
    k_weight,
    v_weight,
    o_weight,
):
    sess_count = lax.axis_size("sess")
    inner_count = lax.axis_size("inner")
    rep_count = lax.axis_size("rep")
    owner_count = sess_count * rep_count
    session_all = speaker_of.shape[0]
    per_device = session_all // (owner_count * inner_count)
    per_owner = per_device * inner_count
    slot_cap = SLOTS // owner_count
    inner_place = lax.axis_index("inner")
    shard_place = lax.axis_index("sess")
    row_owner = row_session[:, 0]
    device_of = row_owner // per_device
    target = (
        (device_of // (inner_count * rep_count) * rep_count + device_of % rep_count) * per_owner
        + device_of // rep_count % inner_count * per_device
        + row_owner % per_device
    )
    row_order = jnp.arange(row_owner.shape[0])
    earlier = jnp.sum(
        (
            (row_owner[:, None] == row_owner[None, :]) & (row_order[None, :] < row_order[:, None])
        ).astype(jnp.int32),
        axis=1,
    )
    slot_place = target * slot_cap + earlier
    counts = jnp.sum(
        (target[:, None] == jnp.arange(owner_count * per_owner)[None, :]).astype(jnp.int32), axis=0
    ).reshape(owner_count, per_owner)
    partial_sum = jnp.dot(thinker_rows, proj_weight, preferred_element_type=jnp.float32)
    own_columns = lax.psum_scatter(partial_sum, "inner", scatter_dimension=1, tiled=True).astype(
        jnp.bfloat16
    )
    buffer = (
        jnp.zeros((owner_count * per_owner * slot_cap, own_columns.shape[1]), own_columns.dtype)
        .at[slot_place]
        .set(own_columns)
    )
    arrived = lax.all_to_all(
        buffer.reshape(owner_count, per_owner * slot_cap, own_columns.shape[1]),
        ("sess", "rep"),
        split_axis=0,
        concat_axis=0,
        tiled=True,
    )
    counts_in = lax.all_to_all(counts, ("sess", "rep"), split_axis=0, concat_axis=0, tiled=True)
    arrived_rows = arrived.reshape(owner_count, per_owner, slot_cap, arrived.shape[2])
    regrouped = lax.all_to_all(arrived_rows, "inner", split_axis=1, concat_axis=3, tiled=True)
    projected = jnp.transpose(regrouped, (1, 0, 2, 3)).reshape(
        per_device, owner_count * slot_cap, regrouped.shape[3]
    )
    own_counts = lax.dynamic_slice_in_dim(counts_in, inner_place * per_device, per_device, 1)
    offsets = jnp.cumsum(own_counts, axis=0) - own_counts
    lengths = jnp.sum(own_counts, axis=0)
    within = jnp.arange(slot_cap)
    position = jnp.transpose(offsets)[:, :, None] + within[None, None, :]
    live_slot = within[None, None, :] < jnp.transpose(own_counts)[:, :, None]
    position = jnp.where(live_slot, position, SLOTS).reshape(per_device, owner_count * slot_cap)
    session_rows = jnp.broadcast_to(jnp.arange(per_device)[:, None], position.shape)
    compact = (
        jnp.zeros((per_device, SLOTS, projected.shape[2]), jnp.bfloat16)
        .at[session_rows, position]
        .set(projected, mode="drop")
    )
    shard_sessions = per_device * inner_count * rep_count
    wanted_speaker = lax.dynamic_slice_in_dim(
        speaker_of, shard_place * shard_sessions, shard_sessions
    )
    speaker_table = jnp.arange(prompt_slot.shape[0])
    wanted_slot = jnp.sum(
        jnp.where(wanted_speaker[:, None] == speaker_table[None, :], prompt_slot[None, :], 0),
        axis=1,
    )
    piece = lax.all_gather(prompt_cache, "sess", axis=0, tiled=True)
    matching = (wanted_slot[:, None] == jnp.arange(piece.shape[0])[None, :]).astype(jnp.bfloat16)
    chosen = jnp.einsum("sp,ptc->stc", matching, piece, preferred_element_type=jnp.float32)
    prompts = lax.all_to_all(
        chosen.astype(jnp.bfloat16), ("inner", "rep"), split_axis=0, concat_axis=1, tiled=True
    )
    summed = attend(compact, lengths, prompts, attn_gain, q_weight, k_weight, v_weight, o_weight)
    live_rows = (jnp.arange(SLOTS)[None, :] < lengths[:, None]).reshape(-1, 1)
    return (
        jnp.where(live_rows, summed, 0.0)
        .astype(jnp.bfloat16)
        .reshape(per_device, SLOTS, summed.shape[1])
    )


def solution(mesh):
    in_specs = (
        P(("groups", "sess", "rep"), "inner"),
        P(("groups", "sess", "rep"), None),
        P("groups"),
        P("groups"),
        P(("groups", "sess"), ("inner", "rep"), None),
        P("inner", None),
        P(),
        P(),
        P(),
        P(),
        P(),
    )
    out_specs = P(("groups", "sess", "inner", "rep"), None, None)
    return jax.shard_map(body, mesh=mesh, in_specs=in_specs, out_specs=out_specs, check_vma=False)
```

profile of v0, /device:TPU:0, one launch (start us, length us, event | category | flops | bytes accessed | tf_op | source)
XLA Modules:
  0.0 214.4 jit_solution(5181493876565836849)
XLA Ops:
  9.3 3.5 %fusion.175 = f32[256,896]{0,1:T(8,128)} fusion(bf16[256,1792]{1,0:T(8,128)(2,1)} %param.11, bf16[1792,896]{1,0:T(8,128)(2,1)S(1)} %copy-done), kind=kOutput, calls=%fused_computation.189 | convolution fusion | flops 822083584 | bytes 5046272 | tf_op jit(solution)/shard_map/dot_general | solution.py:142
  14.4 6.3 %all-to-all-start = ((s32[8,1,4]{2,1,0:T(1,128)}), s32[8,1,4]{2,1,0:T(1,128)S(1)}, u32[]{:S(2)}, u32[]{:S(2)}) async-start(s32[8,1,4]{2,1,0:T(1,128)} %bitcast.1), calls=%async_computation | async-start | bytes 8192 | tf_op jit(solution)/shard_map/all_to_all | solution.py:158
  20.7 4.9 %copy.90 = bf16[896,1536]{0,1:T(8,128)(2,1)} copy(bf16[896,1536]{1,0:T(8,128)(2,1)} %param.18) | data formatting | bytes 5505024 | tf_op args[7]
  29.3 5.2 %reduce-scatter.2.cloned.1.call-done = f32[256,448]{0,1:T(8,128)} async-done(((f32[256,896]{0,1:T(8,128)}), f32[256,448]{0,1:T(8,128)}) %reduce-scatter.2.cloned.1.call-update) | async-done | bytes 458768 | tf_op jit(solution)/shard_map/reduce_scatter | solution.py:143
  38.0 4.6 %all-to-all-start.1 = ((bf16[8,48,448]{2,1,0:T(8,128)(2,1)}), bf16[8,48,448]{2,1,0:T(8,128)(2,1)S(1)}, u32[]{:S(2)}, u32[]{:S(2)}) async-start(bf16[8,48,448]{2,1,0:T(8,128)(2,1)} %bitcast.8), calls=%async_computation.2 | async-start | bytes 786432 | tf_op jit(solution)/shard_map/all_to_all | solution.py:151
  43.7 24.4 %all-to-all-done.1 = bf16[8,48,448]{2,1,0:T(8,128)(2,1)S(1)} async-done(((bf16[8,48,448]{2,1,0:T(8,128)(2,1)}), bf16[8,48,448]{2,1,0:T(8,128)(2,1)S(1)}, u32[]{:S(2)}, u32[]{:S(2)}) %all-to-all-start.1) | async-done | bytes 344096 | tf_op jit(solution)/shard_map/all_to_all | solution.py:151
  69.1 3.5 %all-to-all-start.2 = ((bf16[8,4,12,448]{3,0,2,1:T(8,128)(2,1)}), bf16[8,4,12,448]{3,0,2,1:T(8,128)(2,1)S(1)}, u32[]{:S(2)}, u32[]{:S(2)}) async-start(bf16[8,4,12,448]{3,0,2,1:T(8,128)(2,1)} %bitcast.9), calls=%async_computation.3 | async-start | bytes 786432 | tf_op jit(solution)/shard_map/all_to_all | solution.py:160
  72.5 33.9 %all-gather.2.cloned.1.call-done = bf16[8,256,1024]{2,1,0:T(8,128)(2,1)} async-done(((bf16[2,256,1024]{2,1,0:T(8,128)(2,1)}), bf16[8,256,1024]{2,1,0:T(8,128)(2,1)}) %all-gather.2.cloned.1.call-update) | async-done | bytes 4194320 | tf_op jit(solution)/shard_map/all_gather | solution.py:186
  106.4 4.7 %fusion.22 = bf16[8,256,1024]{2,0,1:T(8,128)(2,1)S(1)} fusion(bf16[8,256,1024]{2,1,0:T(8,128)(2,1)} %all-gather.2.cloned.1.call-done, s32[8]{0:T(128)S(1)} %select_reduce_fusion), kind=kOutput, calls=%fused_computation.34 | convolution fusion | flops 35651648 | bytes 8388640 | tf_op jit(solution)/shard_map/sp,ptc->stc/dot_general | solution.py:188
  111.2 4.3 %copy.80 = bf16[8,256,1024]{2,1,0:T(8,128)(2,1)} copy(bf16[8,256,1024]{2,0,1:T(8,128)(2,1)S(1)} %fusion.22) | data formatting | bytes 8388608 | tf_op jit(solution)/shard_map/convert_element_type | solution.py:190
  115.4 5.0 %all-to-all-start.3 = ((bf16[8,256,1024]{2,1,0:T(8,128)(2,1)}), bf16[8,256,1024]{2,1,0:T(8,128)(2,1)}, u32[]{:S(2)}, u32[]{:S(2)}) async-start(bf16[8,256,1024]{2,1,0:T(8,128)(2,1)} %copy.80), calls=%async_computation.4 | async-start | bytes 8388608 | tf_op jit(solution)/shard_map/all_to_all | solution.py:189
  122.3 13.1 %scatter_fusion = bf16[2,96,896]{2,1,0:T(8,128)(2,1)S(1)} fusion(bf16[2,96,896]{2,1,0:T(8,128)(2,1)S(1)} %broadcast_in_dim.55, s32[192]{0:T(256)S(1)} %reshape.305, bf16[192,896]{1,0:T(8,128)(2,1)S(1)} %reshape.307), kind=kCustom, calls=%fused_computation.1 | custom fusion | bytes 1033728 | tf_op jit(solution)/shard_map/scatter | solution.py:175
  140.3 28.3 %all-to-all-done.3 = bf16[8,256,1024]{2,1,0:T(8,128)(2,1)} async-done(((bf16[8,256,1024]{2,1,0:T(8,128)(2,1)}), bf16[8,256,1024]{2,1,0:T(8,128)(2,1)}, u32[]{:S(2)}, u32[]{:S(2)}) %all-to-all-start.3) | async-done | bytes 4194336 | tf_op jit(solution)/shard_map/all_to_all | solution.py:189
  168.5 2.6 %copy.81 = bf16[2,4,256,1024]{3,2,1,0:T(8,128)(2,1)S(1)} copy(bf16[2,4,256,1024]{3,2,0,1:T(8,128)(2,1)} %bitcast.16) | data formatting | bytes 8388608 | tf_op jit(solution)/shard_map/all_to_all | solution.py:189
  171.1 2.5 %fusion.154 = (bf16[2,1024,512]{2,1,0:T(8,128)(2,1)}, bf16[2,1024,512]{2,1,0:T(8,128)(2,1)}) fusion(bf16[2,1024,1024]{2,1,0:T(8,128)(2,1)S(1)} %bitcast.185), kind=kLoop, calls=%fused_computation.184 | loop fusion | bytes 8388608 | tf_op jit(solution)/shard_map/slice | solution.py:61
  173.6 3.0 %copy.86 = bf16[2,1024,512]{1,2,0:T(8,128)(2,1)S(1)} copy(bf16[2,1024,512]{2,1,0:T(8,128)(2,1)} %get-tuple-element.10) | data formatting | bytes 4194304 | tf_op jit(solution)/shard_map/slice | solution.py:60
  176.7 2.5 %copy.88 = bf16[2,1024,4,128]{3,1,0,2:T(8,128)(2,1)} copy(bf16[2,1024,4,128]{1,3,2,0:T(8,128)(2,1)S(1)} %bitcast.187) | data formatting | bytes 4194304 | tf_op jit(solution)/shard_map/reshape | solution.py:60
  179.2 3.8 %fusion.155 = (f32[2,3,96]{2,1,0:T(4,128)S(1)}, f32[2,3,96,1120]{3,2,1,0:T(8,128)}) fusion(pred[2,96,1120]{2,1,0:T(8,128)(4,1)S(1)} %copy-done.9, bf16[2,1024,4,128]{3,1,0,2:T(8,128)(2,1)} %copy.88, bf16[2,96,12,128]{3,1,2,0:T(8,128)(2,1)S(1)} %fusion.32, bf16[2,96,4,128]{3,1,2,0:T(8,128)(2,1)S(1)} %copy-done.10), kind=kOutput, calls=%fused_computation.185 | convolution fusion | flops 168879200 | bytes 5245184 | tf_op jit(solution)/shard_map/sub | solution.py:81
  183.0 2.6 %fusion.160 = (f32[2,3,96]{2,1,0:T(4,128)S(1)}, f32[2,3,96,1120]{3,2,1,0:T(8,128)}) fusion(pred[2,96,1120]{2,1,0:T(8,128)(4,1)S(1)} %copy-done.9, bf16[2,1024,4,128]{3,1,0,2:T(8,128)(2,1)S(1)} %copy-done.4, bf16[2,96,12,128]{3,1,2,0:T(8,128)(2,1)S(1)} %fusion.32, bf16[2,96,4,128]{3,1,2,0:T(8,128)(2,1)S(1)} %copy-done.10), kind=kOutput, calls=%fused_computation.186 | convolution fusion | flops 168879200 | bytes 5245184 | tf_op jit(solution)/shard_map/sub | solution.py:81
  185.7 2.6 %fusion.165 = (f32[2,3,96]{2,1,0:T(4,128)S(1)}, f32[2,3,96,1120]{3,2,1,0:T(8,128)}) fusion(pred[2,96,1120]{2,1,0:T(8,128)(4,1)S(1)} %copy-done.9, bf16[2,1024,4,128]{3,1,0,2:T(8,128)(2,1)S(1)} %copy-done.4, bf16[2,96,12,128]{3,1,2,0:T(8,128)(2,1)S(1)} %fusion.32, bf16[2,96,4,128]{3,1,2,0:T(8,128)(2,1)S(1)} %copy-done.10), kind=kOutput, calls=%fused_computation.187 | convolution fusion | flops 168879200 | bytes 5245184 | tf_op jit(solution)/shard_map/sub | solution.py:81
  188.3 2.7 %fusion.170 = (f32[2,3,96]{2,1,0:T(4,128)S(1)}, f32[2,3,96,1120]{3,2,1,0:T(8,128)}) fusion(pred[2,96,1120]{2,1,0:T(8,128)(4,1)S(1)} %copy-done.9, bf16[2,1024,4,128]{3,1,0,2:T(8,128)(2,1)S(1)} %copy-done.4, bf16[2,96,12,128]{3,1,2,0:T(8,128)(2,1)S(1)} %fusion.32, bf16[2,96,4,128]{3,1,2,0:T(8,128)(2,1)S(1)} %copy-done.10), kind=kOutput, calls=%fused_computation.188 | convolution fusion | flops 168879200 | bytes 5245184 | tf_op jit(solution)/shard_map/sub | solution.py:81
  190.9 3.0 %copy.82 = bf16[2,1024,512]{1,2,0:T(8,128)(2,1)S(1)} copy(bf16[2,1024,512]{2,1,0:T(8,128)(2,1)} %get-tuple-element.9) | data formatting | bytes 4194304 | tf_op jit(solution)/shard_map/slice | solution.py:61
  193.9 2.9 %copy.84 = bf16[2,1024,4,128]{3,1,0,2:T(8,128)(2,1)} copy(bf16[2,1024,4,128]{1,3,2,0:T(8,128)(2,1)S(1)} %bitcast.188) | data formatting | bytes 4194304 | tf_op jit(solution)/shard_map/reshape | solution.py:61
  196.8 2.6 %fusion.40 = bf16[2,96,3,128]{3,1,2,0:T(8,128)(2,1)S(1)} fusion(f32[2,3,96,1120]{3,2,1,0:T(8,128)} %get-tuple-element.18, f32[2,3,96]{2,1,0:T(4,128)S(1)} %get-tuple-element.17, bf16[2,1024,4,128]{3,1,0,2:T(8,128)(2,1)} %copy.84, bf16[2,96,4,128]{3,1,2,0:T(8,128)(2,1)S(1)} %copy-done.17), kind=kOutput, calls=%fused_computation.64 | convolution fusion | flops 167661568 | bytes 5024000 | tf_op jit(solution)/shard_map/chqk,ckd->cqhd/dot_general | solution.py:84
  (104 shorter events, 26.7 us)
Async XLA Ops:
  7.4 1.9 copy-start
  7.4 6.0 %copy-start.11 = (s32[256,1]{0,1:T(1,128)S(1)}, s32[256,1]{0,1:T(1,128)}, u32[]{:S(2)}) copy-start(s32[256,1]{0,1:T(1,128)} %param.12) | copy-start | bytes 3076
  7.4 27.1 %reduce-scatter.2.cloned.1.call-start = ((), (), s32[]{:S(2)}) async-start(), calls=%async_computation.5 | async-start | bytes 1376256 | tf_op jit(solution)/shard_map/reduce_scatter | solution.py:143
  12.8 93.7 %all-gather.2.cloned.1.call-start = ((), (), s32[]{:S(2)}) async-start(), calls=%async_computation.6 | async-start | bytes 5242880 | tf_op jit(solution)/shard_map/all_gather | solution.py:186
  14.4 14.6 %all-to-all-start = ((s32[8,1,4]{2,1,0:T(1,128)}), s32[8,1,4]{2,1,0:T(1,128)S(1)}, u32[]{:S(2)}, u32[]{:S(2)}) async-start(s32[8,1,4]{2,1,0:T(1,128)} %bitcast.1), calls=%async_computation | async-start | bytes 8192 | tf_op jit(solution)/shard_map/all_to_all | solution.py:158
  20.7 5.0 %copy-start.12 = (bf16[896]{0:T(1024)(128)(2,1)S(1)}, bf16[896]{0:T(1024)(128)(2,1)}, u32[]{:S(2)}) copy-start(bf16[896]{0:T(1024)(128)(2,1)} %param.17) | copy-start | bytes 5380
  20.7 5.0 %copy-start.5 = (bf16[896,512]{1,0:T(8,128)(2,1)S(1)}, bf16[896,512]{1,0:T(8,128)(2,1)}, u32[]{:S(2)}) copy-start(bf16[896,512]{1,0:T(8,128)(2,1)} %param.19) | copy-start | bytes 2752516
  20.7 5.6 %copy-start.14 = (s32[32]{0:T(128)S(1)}, s32[32]{0:T(128)}, u32[]{:S(2)}) copy-start(s32[32]{0:T(128)} %param.13) | copy-start | bytes 388
  20.7 5.7 %copy-start.15 = (s32[8]{0:T(128)S(1)}, s32[8]{0:T(128)}, u32[]{:S(2)}) copy-start(s32[8]{0:T(128)} %param.14) | copy-start | bytes 100
  25.6 2.1 copy-start.6
  38.0 30.1 %all-to-all-start.1 = ((bf16[8,48,448]{2,1,0:T(8,128)(2,1)}), bf16[8,48,448]{2,1,0:T(8,128)(2,1)S(1)}, u32[]{:S(2)}, u32[]{:S(2)}) async-start(bf16[8,48,448]{2,1,0:T(8,128)(2,1)} %bitcast.8), calls=%async_computation.2 | async-start | bytes 786432 | tf_op jit(solution)/shard_map/all_to_all | solution.py:151
  69.1 46.4 %all-to-all-start.2 = ((bf16[8,4,12,448]{3,0,2,1:T(8,128)(2,1)}), bf16[8,4,12,448]{3,0,2,1:T(8,128)(2,1)S(1)}, u32[]{:S(2)}, u32[]{:S(2)}) async-start(bf16[8,4,12,448]{3,0,2,1:T(8,128)(2,1)} %bitcast.9), calls=%async_computation.3 | async-start | bytes 786432 | tf_op jit(solution)/shard_map/all_to_all | solution.py:160
  115.4 53.1 %all-to-all-start.3 = ((bf16[8,256,1024]{2,1,0:T(8,128)(2,1)}), bf16[8,256,1024]{2,1,0:T(8,128)(2,1)}, u32[]{:S(2)}, u32[]{:S(2)}) async-start(bf16[8,256,1024]{2,1,0:T(8,128)(2,1)} %copy.80), calls=%async_computation.4 | async-start | bytes 8388608 | tf_op jit(solution)/shard_map/all_to_all | solution.py:189
  136.0 2.2 %copy-start.2 = (bf16[896,1536]{0,1:T(8,128)(2,1)S(1)}, bf16[896,1536]{0,1:T(8,128)(2,1)}, u32[]{:S(2)}) copy-start(bf16[896,1536]{0,1:T(8,128)(2,1)} %copy.90) | copy-start | bytes 8257540
  176.6 2.6 %copy-start.9 = (pred[2,96,1120]{2,1,0:T(8,128)(4,1)S(1)}, pred[2,96,1120]{2,1,0:T(8,128)(4,1)}, u32[]{:S(2)}) copy-start(pred[2,96,1120]{2,1,0:T(8,128)(4,1)} %and_or_fusion) | copy-start | bytes 645124
  176.6 2.6 %copy-start.10 = (bf16[2,96,4,128]{3,1,2,0:T(8,128)(2,1)S(1)}, bf16[2,96,4,128]{3,1,2,0:T(8,128)(2,1)}, u32[]{:S(2)}) copy-start(bf16[2,96,4,128]{3,1,2,0:T(8,128)(2,1)} %fusion.68) | copy-start | bytes 589828
  179.2 3.8 %copy-start.4 = (bf16[2,1024,4,128]{3,1,0,2:T(8,128)(2,1)S(1)}, bf16[2,1024,4,128]{3,1,0,2:T(8,128)(2,1)}, u32[]{:S(2)}) copy-start(bf16[2,1024,4,128]{3,1,0,2:T(8,128)(2,1)} %copy.88) | copy-start | bytes 6291460
  193.9 2.9 %copy-start.17 = (bf16[2,96,4,128]{3,1,2,0:T(8,128)(2,1)S(1)}, bf16[2,96,4,128]{3,1,2,0:T(8,128)(2,1)}, u32[]{:S(2)}) copy-start(bf16[2,96,4,128]{3,1,2,0:T(8,128)(2,1)} %convolution_convert_fusion) | copy-start | bytes 589828
  196.8 2.6 %copy-start.3 = (bf16[2,1024,4,128]{3,1,0,2:T(8,128)(2,1)S(1)}, bf16[2,1024,4,128]{3,1,0,2:T(8,128)(2,1)}, u32[]{:S(2)}) copy-start(bf16[2,1024,4,128]{3,1,0,2:T(8,128)(2,1)} %copy.84) | copy-start | bytes 6291460
  196.8 3.3 %copy-start.20 = (f32[2,3,96,1120]{3,2,1,0:T(8,128)S(1)}, f32[2,3,96,1120]{3,2,1,0:T(8,128)}, u32[]{:S(2)}) copy-start(f32[2,3,96,1120]{3,2,1,0:T(8,128)} %get-tuple-element.20) | copy-start | bytes 7741444
  200.1 1.7 copy-start.19
  201.9 1.7 copy-start.18
  203.6 1.8 copy-start.13
  204.6 2.4 %copy-start.1 = (bf16[1792,896]{1,0:T(8,128)(2,1)S(1)}, bf16[1792,896]{1,0:T(8,128)(2,1)}, u32[]{:S(2)}) copy-start(bf16[1792,896]{1,0:T(8,128)(2,1)} %param.16) | copy-start | bytes 9633796
  (3 other events, 3.6 us)
Sparse Core Ops, SparseCore 0:
  12.9 21.5 reduce-scatter.1
Sparse Core Ops, SparseCore 1:
  14.8 91.6 all-gather.1
where the time goes:
time: 215 us; the launch traced here: 214 us
  waiting for transfers between devices  92.3 us (43%)
  local copies, waits for them, and re-layouts  52.8 us (25%)
  matrix products  28.5 us (13%)
  starting transfers between devices  19.5 us (9%)
  between operations  15.2 us (7%)
  other arithmetic  6.03 us (3%)
    all_gather x1, waiting for transfers between devices, body(): piece = lax.all_gather(prompt_cache, 'sess', axis=0, tiled=True)  33.9 us
    all_to_all x1, waiting for transfers between devices, body(): lax.all_to_all(chosen.astype(jnp.bfloat16), ('inner', 'rep'), split_axis=...  28.3 us
    all_to_all x1, waiting for transfers between devices, body(): lax.all_to_all(buffer.reshape(owner_count, per_owner * slot_cap, own_colu...  24.4 us
    scatter x1, local copies, waits for them, and re-layouts, body(): compact = jnp.zeros((per_device, SLOTS, projected.shape[2]), jnp.bfloat16...  13.1 us
    sub x4, matrix products, attend(): powers = jnp.exp(scores - highest)  11.7 us
    unnamed x43, local copies, waits for them, and re-layouts  10.7 us
    all_to_all x1, starting transfers between devices, body(): lax.all_to_all(counts, ('sess', 'rep'), split_axis=0, concat_axis=0, tile...  6.33 us
    slice x2, local copies, waits for them, and re-layouts, attend(): prompts[:, :, KVH * HD:].reshape(session_total, PROMPT, KVH, HD)  5.48 us
  transfers between devices with their start and end apart: 6, of which 4 were waited for; matrix products, arithmetic and copies ran while one was open for 20% of the time, Pallas kernels for 0%

commit v1 on v0

--- a/solution.py
+++ b/solution.py
@@ -10,6 +10,28 @@
 SLOTS = 96
 EPSILON = 1e-06
 ROPE_BASE = 1000000.0
+
+
+def in_order(blocks, dim):
+    shape = list(blocks.shape[1:])
+    shape[dim] *= blocks.shape[0]
+    return jnp.moveaxis(blocks, 0, dim).reshape(shape)
+
+
+def gather_around(x, axis, dim):
+    devices = lax.axis_size(axis)
+    pairs = [(i, (i + 1) % devices) for i in range(devices)]
+    back = [(b, a) for a, b in pairs]
+    lower, upper = ([], [])
+    for step in range(devices - 1):
+        if step % 2 == 0:
+            lower.append(lax.ppermute(lower[-1] if lower else x, axis, pairs))
+        else:
+            upper.append(lax.ppermute(upper[-1] if upper else x, axis, back))
+    blocks = jnp.stack([*lower[::-1], x, *upper])
+    shift = lax.axis_index(axis) - len(lower)
+    blocks = blocks[(jnp.arange(devices) - shift) % devices]
+    return in_order(blocks, dim)
 
 
 def rms_scale(states, gain):
@@ -183,7 +205,7 @@
         jnp.where(wanted_speaker[:, None] == speaker_table[None, :], prompt_slot[None, :], 0),
         axis=1,
     )
-    piece = lax.all_gather(prompt_cache, "sess", axis=0, tiled=True)
+    piece = gather_around(prompt_cache, "sess", 0)
     matching = (wanted_slot[:, None] == jnp.arange(piece.shape[0])[None, :]).astype(jnp.bfloat16)
     chosen = jnp.einsum("sp,ptc->stc", matching, piece, preferred_element_type=jnp.float32)
     prompts = lax.all_to_all(

time: 215 us -> 207 us (0.963)
  waiting for transfers between devices: 92.3 us -> 72.6 us
  other arithmetic: 6.03 us -> 11.1 us
  starting transfers between devices: 19.5 us -> 23.8 us
  local copies, waits for them, and re-layouts: 52.8 us -> 56.6 us
    ppermute x0 -> x3, waiting for transfers between devices: none -> 44.3 us  [the longest x2 44.3 us: gather_around(): lower.append(lax.ppermute(lower[-1] if lower else x, axis, pairs))]
    all_gather x1 -> x0, waiting for transfers between devices: 33.9 us -> none  [body(): piece = lax.all_gather(prompt_cache, 'sess', axis=0, tiled=True)]
    all_to_all x1, waiting for transfers between devices: 24.4 us -> 0.01 us  [body(): lax.all_to_all(buffer.reshape(owner_count, per_owner * slot_cap, own_colu...]
    ppermute x0 -> x3, starting transfers between devices: none -> 6.67 us  [the longest x1 5.05 us: gather_around(): upper.append(lax.ppermute(upper[-1] if upper else x, axis, back))]
    reduce_scatter x1, waiting for transfers between devices: 5.19 us -> 0.01 us  [body(): lax.psum_scatter(partial_sum, 'inner', scatter_dimension=1, tiled=True)]
    gather x0 -> x1, local copies, waits for them, and re-layouts: none -> 4.97 us  [gather_around(): blocks = blocks[(jnp.arange(devices) - shift) % devices]]
    another operation x0 -> x1, other arithmetic: none -> 3.58 us  [gather_around(): blocks = jnp.stack([*lower[::-1], x, *upper])]
    unnamed x43 -> x41, local copies, waits for them, and re-layouts: 10.7 us -> 8.63 us
  transfers between devices with their start and end apart: 6 -> 8, of which waited for: 4 -> 3; matrix products, arithmetic and copies ran while one was open for 20% -> 27% of each run, Pallas kernels for 0% -> 0%
where the time goes in v1:
time: 207 us; the launch traced here: 206 us
  waiting for transfers between devices  72.6 us (35%)
  local copies, waits for them, and re-layouts  56.6 us (27%)
  matrix products  28.5 us (14%)
  starting transfers between devices  23.8 us (11%)
  between operations  13.8 us (7%)
  other arithmetic  11.1 us (5%)
    ppermute x2, waiting for transfers between devices, gather_around(): lower.append(lax.ppermute(lower[-1] if lower else x, axis, pairs))  44.3 us
    all_to_all x1, waiting for transfers between devices, body(): lax.all_to_all(chosen.astype(jnp.bfloat16), ('inner', 'rep'), split_axis=...  28.3 us
    scatter x1, local copies, waits for them, and re-layouts, body(): compact = jnp.zeros((per_device, SLOTS, projected.shape[2]), jnp.bfloat16...  13.1 us
    sub x4, matrix products, attend(): powers = jnp.exp(scores - highest)  11.7 us
    unnamed x41, local copies, waits for them, and re-layouts  8.63 us
    slice x2, local copies, waits for them, and re-layouts, attend(): prompts[:, :, KVH * HD:].reshape(session_total, PROMPT, KVH, HD)  5.48 us
    all_to_all x1, starting transfers between devices, body(): lax.all_to_all(counts, ('sess', 'rep'), split_axis=0, concat_axis=0, tile...  5.1 us
    ppermute x1, starting transfers between devices, gather_around(): upper.append(lax.ppermute(upper[-1] if upper else x, axis, back))  5.05 us
  transfers between devices with their start and end apart: 8, of which 3 were waited for; matrix products, arithmetic and copies ran while one was open for 27% of the time, Pallas kernels for 0%

profile of v1, /device:TPU:0, one launch (start us, length us, event | category | flops | bytes accessed | tf_op | source)
XLA Modules:
  0.0 206.3 jit_solution(15311245794595788445)
XLA Ops:
  6.5 5.0 %collective-permute-start.2 = (bf16[2,256,1024]{2,1,0:T(8,128)(2,1)}, bf16[2,256,1024]{2,1,0:T(8,128)(2,1)}, u32[]{:S(2)}, u32[]{:S(2)}) collective-permute-start(bf16[2,256,1024]{2,1,0:T(8,128)(2,1)} %param.15), channel_id=1, source_target_pairs={{4,0},{8,4},{12,8},{0,12},{5,1},{9,5},{13,9},{1,13},{6,2},{10,6},{... | collective-permute-start | bytes 3145736 | tf_op jit(solution)/shard_map/ppermute | solution.py:30
  14.0 5.1 %all-to-all-start = ((s32[8,1,4]{2,1,0:T(1,128)}), s32[8,1,4]{2,1,0:T(1,128)S(1)}, u32[]{:S(2)}, u32[]{:S(2)}) async-start(s32[8,1,4]{2,1,0:T(1,128)} %bitcast.1), calls=%async_computation | async-start | bytes 8192 | tf_op jit(solution)/shard_map/all_to_all | solution.py:180
  19.2 3.5 %fusion.177 = f32[256,896]{0,1:T(8,128)} fusion(bf16[256,1792]{1,0:T(8,128)(2,1)} %param.11, bf16[1792,896]{1,0:T(8,128)(2,1)S(1)} %copy-done), kind=kOutput, calls=%fused_computation.198 | convolution fusion | flops 822083584 | bytes 5046272 | tf_op jit(solution)/shard_map/dot_general | solution.py:164
  23.1 34.7 %collective-permute-done = bf16[2,256,1024]{2,1,0:T(8,128)(2,1)} collective-permute-done((bf16[2,256,1024]{2,1,0:T(8,128)(2,1)}, bf16[2,256,1024]{2,1,0:T(8,128)(2,1)}, u32[]{:S(2)}, u32[]{:S(2)}) %collective-permute-start) | collective-permute-done | bytes 1048608 | tf_op jit(solution)/shard_map/ppermute | solution.py:28
  59.4 4.7 %copy.90 = bf16[896,1536]{0,1:T(8,128)(2,1)} copy(bf16[896,1536]{1,0:T(8,128)(2,1)} %param.18) | data formatting | bytes 5505024 | tf_op args[7]
  72.1 3.5 %all-to-all-start.1 = ((bf16[8,48,448]{2,1,0:T(8,128)(2,1)}), bf16[8,48,448]{2,1,0:T(8,128)(2,1)S(1)}, u32[]{:S(2)}, u32[]{:S(2)}) async-start(bf16[8,48,448]{2,1,0:T(8,128)(2,1)} %bitcast.8), calls=%async_computation.2 | async-start | bytes 786432 | tf_op jit(solution)/shard_map/all_to_all | solution.py:173
  76.3 9.6 %collective-permute-done.1 = bf16[2,256,1024]{2,1,0:T(8,128)(2,1)} collective-permute-done((bf16[2,256,1024]{2,1,0:T(8,128)(2,1)}, bf16[2,256,1024]{2,1,0:T(8,128)(2,1)}, u32[]{:S(2)}, u32[]{:S(2)}) %collective-permute-start.1) | collective-permute-done | bytes 1048608 | tf_op jit(solution)/shard_map/ppermute | solution.py:28
  86.0 3.6 %pad_maximum_fusion = bf16[4,2,256,1024]{3,2,1,0:T(8,128)(2,1)} fusion(bf16[1,2,256,1024]{3,2,1,0:T(8,128)(2,1)} %bitcast.18, bf16[1,2,256,1024]{3,2,1,0:T(8,128)(2,1)S(1)} %bitcast.200, bf16[1,2,256,1024]{3,2,1,0:T(8,128)(2,1)} %bitcast.16, bf16[1,2,256,1024]{3,2,1,0:T(8,128)(2,1)} %bitcast.15), kind=kLoop, calls=%fused_computation.7 | loop fusion | flops 6291456 | bytes 8388608 | tf_op jit(solution)/shard_map/stack | solution.py:31
  89.6 5.0 %gather_fusion = bf16[4,2,256,1024]{3,2,1,0:T(8,128)(2,1)} fusion(bf16[4,2,256,1024]{3,2,1,0:T(8,128)(2,1)} %pad_maximum_fusion, s32[1024]{0:T(1024)S(1)} %pad_clamp_fusion), kind=kCustom, calls=%fused_computation | custom fusion | bytes 8388624 | tf_op jit(solution)/shard_map/gather | solution.py:33
  95.5 3.5 %all-to-all-start.2 = ((bf16[8,4,12,448]{3,0,2,1:T(8,128)(2,1)}), bf16[8,4,12,448]{3,0,2,1:T(8,128)(2,1)S(1)}, u32[]{:S(2)}, u32[]{:S(2)}) async-start(bf16[8,4,12,448]{3,0,2,1:T(8,128)(2,1)} %bitcast.9), calls=%async_computation.3 | async-start | bytes 786432 | tf_op jit(solution)/shard_map/all_to_all | solution.py:182
  99.0 4.7 %fusion.22 = bf16[8,256,1024]{2,0,1:T(8,128)(2,1)S(1)} fusion(bf16[8,256,1024]{2,1,0:T(8,128)(2,1)} %bitcast.192, s32[8]{0:T(128)S(1)} %select_reduce_fusion), kind=kOutput, calls=%fused_computation.36 | convolution fusion | flops 35651648 | bytes 8388640 | tf_op jit(solution)/shard_map/sp,ptc->stc/dot_general | solution.py:210
  103.7 4.3 %copy.80 = bf16[8,256,1024]{2,1,0:T(8,128)(2,1)} copy(bf16[8,256,1024]{2,0,1:T(8,128)(2,1)S(1)} %fusion.22) | data formatting | bytes 8388608 | tf_op jit(solution)/shard_map/convert_element_type | solution.py:212
  108.0 5.0 %all-to-all-start.3 = ((bf16[8,256,1024]{2,1,0:T(8,128)(2,1)}), bf16[8,256,1024]{2,1,0:T(8,128)(2,1)}, u32[]{:S(2)}, u32[]{:S(2)}) async-start(bf16[8,256,1024]{2,1,0:T(8,128)(2,1)} %copy.80), calls=%async_computation.4 | async-start | bytes 8388608 | tf_op jit(solution)/shard_map/all_to_all | solution.py:211
  114.8 13.1 %scatter_fusion = bf16[2,96,896]{2,1,0:T(8,128)(2,1)S(1)} fusion(bf16[2,96,896]{2,1,0:T(8,128)(2,1)S(1)} %broadcast_in_dim.55, s32[192]{0:T(256)S(1)} %reshape.366, bf16[192,896]{1,0:T(8,128)(2,1)S(1)} %reshape.368), kind=kCustom, calls=%fused_computation.2 | custom fusion | bytes 1033728 | tf_op jit(solution)/shard_map/scatter | solution.py:197
  132.8 28.3 %all-to-all-done.3 = bf16[8,256,1024]{2,1,0:T(8,128)(2,1)} async-done(((bf16[8,256,1024]{2,1,0:T(8,128)(2,1)}), bf16[8,256,1024]{2,1,0:T(8,128)(2,1)}, u32[]{:S(2)}, u32[]{:S(2)}) %all-to-all-start.3) | async-done | bytes 4194336 | tf_op jit(solution)/shard_map/all_to_all | solution.py:211
  161.1 2.6 %copy.81 = bf16[2,4,256,1024]{3,2,1,0:T(8,128)(2,1)S(1)} copy(bf16[2,4,256,1024]{3,2,0,1:T(8,128)(2,1)} %bitcast.22) | data formatting | bytes 8388608 | tf_op jit(solution)/shard_map/all_to_all | solution.py:211
  166.2 3.0 %copy.86 = bf16[2,1024,512]{1,2,0:T(8,128)(2,1)S(1)} copy(bf16[2,1024,512]{2,1,0:T(8,128)(2,1)} %get-tuple-element.10) | data formatting | bytes 4194304 | tf_op jit(solution)/shard_map/slice | solution.py:82
  171.8 3.8 %fusion.157 = (f32[2,3,96]{2,1,0:T(4,128)S(1)}, f32[2,3,96,1120]{3,2,1,0:T(8,128)}) fusion(pred[2,96,1120]{2,1,0:T(8,128)(4,1)S(1)} %copy-done.9, bf16[2,1024,4,128]{3,1,0,2:T(8,128)(2,1)} %copy.88, bf16[2,96,12,128]{3,1,2,0:T(8,128)(2,1)S(1)} %fusion.32, bf16[2,96,4,128]{3,1,2,0:T(8,128)(2,1)S(1)} %copy-done.10), kind=kOutput, calls=%fused_computation.194 | convolution fusion | flops 168879200 | bytes 5245184 | tf_op jit(solution)/shard_map/sub | solution.py:103
  175.6 2.6 %fusion.162 = (f32[2,3,96]{2,1,0:T(4,128)S(1)}, f32[2,3,96,1120]{3,2,1,0:T(8,128)}) fusion(pred[2,96,1120]{2,1,0:T(8,128)(4,1)S(1)} %copy-done.9, bf16[2,1024,4,128]{3,1,0,2:T(8,128)(2,1)S(1)} %copy-done.4, bf16[2,96,12,128]{3,1,2,0:T(8,128)(2,1)S(1)} %fusion.32, bf16[2,96,4,128]{3,1,2,0:T(8,128)(2,1)S(1)} %copy-done.10), kind=kOutput, calls=%fused_computation.195 | convolution fusion | flops 168879200 | bytes 5245184 | tf_op jit(solution)/shard_map/sub | solution.py:103
  178.2 2.6 %fusion.167 = (f32[2,3,96]{2,1,0:T(4,128)S(1)}, f32[2,3,96,1120]{3,2,1,0:T(8,128)}) fusion(pred[2,96,1120]{2,1,0:T(8,128)(4,1)S(1)} %copy-done.9, bf16[2,1024,4,128]{3,1,0,2:T(8,128)(2,1)S(1)} %copy-done.4, bf16[2,96,12,128]{3,1,2,0:T(8,128)(2,1)S(1)} %fusion.32, bf16[2,96,4,128]{3,1,2,0:T(8,128)(2,1)S(1)} %copy-done.10), kind=kOutput, calls=%fused_computation.196 | convolution fusion | flops 168879200 | bytes 5245184 | tf_op jit(solution)/shard_map/sub | solution.py:103
  180.8 2.7 %fusion.172 = (f32[2,3,96]{2,1,0:T(4,128)S(1)}, f32[2,3,96,1120]{3,2,1,0:T(8,128)}) fusion(pred[2,96,1120]{2,1,0:T(8,128)(4,1)S(1)} %copy-done.9, bf16[2,1024,4,128]{3,1,0,2:T(8,128)(2,1)S(1)} %copy-done.4, bf16[2,96,12,128]{3,1,2,0:T(8,128)(2,1)S(1)} %fusion.32, bf16[2,96,4,128]{3,1,2,0:T(8,128)(2,1)S(1)} %copy-done.10), kind=kOutput, calls=%fused_computation.197 | convolution fusion | flops 168879200 | bytes 5245184 | tf_op jit(solution)/shard_map/sub | solution.py:103
  183.5 3.0 %copy.82 = bf16[2,1024,512]{1,2,0:T(8,128)(2,1)S(1)} copy(bf16[2,1024,512]{2,1,0:T(8,128)(2,1)} %get-tuple-element.9) | data formatting | bytes 4194304 | tf_op jit(solution)/shard_map/slice | solution.py:83
  186.5 2.9 %copy.84 = bf16[2,1024,4,128]{3,1,0,2:T(8,128)(2,1)} copy(bf16[2,1024,4,128]{1,3,2,0:T(8,128)(2,1)S(1)} %bitcast.196) | data formatting | bytes 4194304 | tf_op jit(solution)/shard_map/reshape | solution.py:83
  189.3 2.6 %fusion.40 = bf16[2,96,3,128]{3,1,2,0:T(8,128)(2,1)S(1)} fusion(f32[2,3,96,1120]{3,2,1,0:T(8,128)} %get-tuple-element.18, f32[2,3,96]{2,1,0:T(4,128)S(1)} %get-tuple-element.17, bf16[2,1024,4,128]{3,1,0,2:T(8,128)(2,1)} %copy.84, bf16[2,96,4,128]{3,1,2,0:T(8,128)(2,1)S(1)} %copy-done.16), kind=kOutput, calls=%fused_computation.66 | convolution fusion | flops 167661568 | bytes 5024000 | tf_op jit(solution)/shard_map/chqk,ckd->cqhd/dot_general | solution.py:106
  (109 shorter events, 33.4 us)
Async XLA Ops:
  6.5 12.6 %copy-start = (bf16[1792,896]{1,0:T(8,128)(2,1)S(1)}, bf16[1792,896]{1,0:T(8,128)(2,1)}, u32[]{:S(2)}) copy-start(bf16[1792,896]{1,0:T(8,128)(2,1)} %param.16) | copy-start | bytes 9633796
  6.5 69.8 %collective-permute-start.2 = (bf16[2,256,1024]{2,1,0:T(8,128)(2,1)}, bf16[2,256,1024]{2,1,0:T(8,128)(2,1)}, u32[]{:S(2)}, u32[]{:S(2)}) collective-permute-start(bf16[2,256,1024]{2,1,0:T(8,128)(2,1)} %param.15), channel_id=1, source_target_pairs={{4,0},{8,4},{12,8},{0,12},{5,1},{9,5},{13,9},{1,13},{6,2},{10,6},{... | collective-permute-start | bytes 3145736 | tf_op jit(solution)/shard_map/ppermute | solution.py:30
  11.6 46.1 %collective-permute-start = (bf16[2,256,1024]{2,1,0:T(8,128)(2,1)}, bf16[2,256,1024]{2,1,0:T(8,128)(2,1)}, u32[]{:S(2)}, u32[]{:S(2)}) collective-permute-start(bf16[2,256,1024]{2,1,0:T(8,128)(2,1)} %param.15), channel_id=1, source_target_pairs={{0,4},{4,8},{8,12},{12,0},{1,5},{5,9},{9,13},{13,1},{2,6},{6,10},{... | collective-permute-start | bytes 3145736 | tf_op jit(solution)/shard_map/ppermute | solution.py:28
  14.0 53.9 %all-to-all-start = ((s32[8,1,4]{2,1,0:T(1,128)}), s32[8,1,4]{2,1,0:T(1,128)S(1)}, u32[]{:S(2)}, u32[]{:S(2)}) async-start(s32[8,1,4]{2,1,0:T(1,128)} %bitcast.1), calls=%async_computation | async-start | bytes 8192 | tf_op jit(solution)/shard_map/all_to_all | solution.py:180
  19.1 49.5 %reduce-scatter.2.cloned.1.call-start = ((), (), s32[]{:S(2)}) async-start(), calls=%async_computation.5 | async-start | bytes 1376256 | tf_op jit(solution)/shard_map/reduce_scatter | solution.py:165
  57.7 28.3 %collective-permute-start.1 = (bf16[2,256,1024]{2,1,0:T(8,128)(2,1)}, bf16[2,256,1024]{2,1,0:T(8,128)(2,1)}, u32[]{:S(2)}, u32[]{:S(2)}) collective-permute-start(bf16[2,256,1024]{2,1,0:T(8,128)(2,1)} %collective-permute-done), channel_id=1, source_target_pairs={{0,4},{4,8},{8,12},{12,0},{1,5},{5,9},{9,13},{13,1},{2,6},{6,10},{... | collective-permute-start | bytes 3145736 | tf_op jit(solution)/shard_map/ppermute | solution.py:28
  59.4 4.8 %copy-start.11 = (bf16[896]{0:T(1024)(128)(2,1)S(1)}, bf16[896]{0:T(1024)(128)(2,1)}, u32[]{:S(2)}) copy-start(bf16[896]{0:T(1024)(128)(2,1)} %param.17) | copy-start | bytes 5380
  59.4 4.8 %copy-start.6 = (bf16[896,512]{1,0:T(8,128)(2,1)S(1)}, bf16[896,512]{1,0:T(8,128)(2,1)}, u32[]{:S(2)}) copy-start(bf16[896,512]{1,0:T(8,128)(2,1)} %param.19) | copy-start | bytes 2752516
  59.4 5.4 %copy-start.13 = (s32[32]{0:T(128)S(1)}, s32[32]{0:T(128)}, u32[]{:S(2)}) copy-start(s32[32]{0:T(128)} %param.13) | copy-start | bytes 388
  59.4 5.5 %copy-start.14 = (s32[8]{0:T(128)S(1)}, s32[8]{0:T(128)}, u32[]{:S(2)}) copy-start(s32[8]{0:T(128)} %param.14) | copy-start | bytes 100
  64.8 21.2 %copy-start.5 = (bf16[2,256,1024]{2,1,0:T(8,128)(2,1)S(1)}, bf16[2,256,1024]{2,1,0:T(8,128)(2,1)}, u32[]{:S(2)}) copy-start(bf16[2,256,1024]{2,1,0:T(8,128)(2,1)} %param.15) | copy-start | bytes 3145732
  72.1 22.5 %all-to-all-start.1 = ((bf16[8,48,448]{2,1,0:T(8,128)(2,1)}), bf16[8,48,448]{2,1,0:T(8,128)(2,1)S(1)}, u32[]{:S(2)}, u32[]{:S(2)}) async-start(bf16[8,48,448]{2,1,0:T(8,128)(2,1)} %bitcast.8), calls=%async_computation.2 | async-start | bytes 786432 | tf_op jit(solution)/shard_map/all_to_all | solution.py:173
  95.5 12.5 %all-to-all-start.2 = ((bf16[8,4,12,448]{3,0,2,1:T(8,128)(2,1)}), bf16[8,4,12,448]{3,0,2,1:T(8,128)(2,1)S(1)}, u32[]{:S(2)}, u32[]{:S(2)}) async-start(bf16[8,4,12,448]{3,0,2,1:T(8,128)(2,1)} %bitcast.9), calls=%async_computation.3 | async-start | bytes 786432 | tf_op jit(solution)/shard_map/all_to_all | solution.py:182
  108.0 53.1 %all-to-all-start.3 = ((bf16[8,256,1024]{2,1,0:T(8,128)(2,1)}), bf16[8,256,1024]{2,1,0:T(8,128)(2,1)}, u32[]{:S(2)}, u32[]{:S(2)}) async-start(bf16[8,256,1024]{2,1,0:T(8,128)(2,1)} %copy.80), calls=%async_computation.4 | async-start | bytes 8388608 | tf_op jit(solution)/shard_map/all_to_all | solution.py:211
  128.6 2.2 %copy-start.2 = (bf16[896,1536]{0,1:T(8,128)(2,1)S(1)}, bf16[896,1536]{0,1:T(8,128)(2,1)}, u32[]{:S(2)}) copy-start(bf16[896,1536]{0,1:T(8,128)(2,1)} %copy.90) | copy-start | bytes 8257540
  169.2 2.6 %copy-start.9 = (pred[2,96,1120]{2,1,0:T(8,128)(4,1)S(1)}, pred[2,96,1120]{2,1,0:T(8,128)(4,1)}, u32[]{:S(2)}) copy-start(pred[2,96,1120]{2,1,0:T(8,128)(4,1)} %and_or_fusion) | copy-start | bytes 645124
  169.2 2.6 %copy-start.10 = (bf16[2,96,4,128]{3,1,2,0:T(8,128)(2,1)S(1)}, bf16[2,96,4,128]{3,1,2,0:T(8,128)(2,1)}, u32[]{:S(2)}) copy-start(bf16[2,96,4,128]{3,1,2,0:T(8,128)(2,1)} %fusion.68) | copy-start | bytes 589828
  171.8 3.8 %copy-start.4 = (bf16[2,1024,4,128]{3,1,0,2:T(8,128)(2,1)S(1)}, bf16[2,1024,4,128]{3,1,0,2:T(8,128)(2,1)}, u32[]{:S(2)}) copy-start(bf16[2,1024,4,128]{3,1,0,2:T(8,128)(2,1)} %copy.88) | copy-start | bytes 6291460
  186.5 2.9 %copy-start.16 = (bf16[2,96,4,128]{3,1,2,0:T(8,128)(2,1)S(1)}, bf16[2,96,4,128]{3,1,2,0:T(8,128)(2,1)}, u32[]{:S(2)}) copy-start(bf16[2,96,4,128]{3,1,2,0:T(8,128)(2,1)} %convolution_convert_fusion) | copy-start | bytes 589828
  189.3 2.6 %copy-start.3 = (bf16[2,1024,4,128]{3,1,0,2:T(8,128)(2,1)S(1)}, bf16[2,1024,4,128]{3,1,0,2:T(8,128)(2,1)}, u32[]{:S(2)}) copy-start(bf16[2,1024,4,128]{3,1,0,2:T(8,128)(2,1)} %copy.84) | copy-start | bytes 6291460
  189.3 3.3 %copy-start.19 = (f32[2,3,96,1120]{3,2,1,0:T(8,128)S(1)}, f32[2,3,96,1120]{3,2,1,0:T(8,128)}, u32[]{:S(2)}) copy-start(f32[2,3,96,1120]{3,2,1,0:T(8,128)} %get-tuple-element.20) | copy-start | bytes 7741444
  196.2 1.8 copy-start.12
  196.2 1.8 copy-start.15
  197.1 2.4 %copy-start.1 = (bf16[1792,896]{1,0:T(8,128)(2,1)S(1)}, bf16[1792,896]{1,0:T(8,128)(2,1)}, u32[]{:S(2)}) copy-start(bf16[1792,896]{1,0:T(8,128)(2,1)} %param.16) | copy-start | bytes 9633796
  (4 other events, 6.1 us)
Sparse Core Ops, SparseCore 0:
  22.8 20.2 reduce-scatter.1
